TPU v7x, 256 devices: a whole 4x4x8 slice. The times are simulated.
256 devices in a mesh: section: 4 (over y), ctx: 64 (over z, x, core).
Axes of the slice: x: 4, y: 4, z: 8, core: 2. Of those that a mesh axis runs over, the one named last changes fastest.
Arguments:
- incoming: bfloat16 [4, 8192, 4096], P('section', 'ctx'), may hold values from -6 to 6
- layer_input: bfloat16 [4, 8192, 4096], P('section', 'ctx'), may hold values from -6 to 6
- pre_gate: bfloat16 [4, 8192, 4096], P('section', 'ctx'), may hold values from -6 to 6
- mid_gate: bfloat16 [4, 8192, 4096], P('section', 'ctx'), may hold values from -6 to 6
- long_gate: bfloat16 [4, 8192, 4096], P('section', 'ctx'), may hold values from -6 to 6
- out_gate: bfloat16 [4, 8192, 4096], P('section', 'ctx'), may hold values from -6 to 6
- long_filter: bfloat16 [4, 4096, 8192], P('section', 'ctx'), may hold values from -0.0625 to 0.0625
- mid_filter: bfloat16 [4, 128, 4096], P('section'), may hold values from -0.5 to 0.5
Outputs:
- input_grad: bfloat16 [4, 8192, 4096], P('section', 'ctx')
- long_grad: bfloat16 [4, 4096, 8192], P('section', 'ctx')
- mid_grad: bfloat16 [4, 128, 4096], P('section', None, 'ctx')
All inputs are finite; a program needn't handle non-finite values.
Results may differ from a plain program's by a relative error of at most 0.008.
Values may be sent and summed in bfloat16 or wider, within the bound.
A program may use at most 192 MiB of HBM per device.

v0:
```python
import math

import jax
import jax.numpy as jnp
from jax import lax
from jax.sharding import PartitionSpec as P


def passed_along(value, axis, steps):
    count = lax.axis_size(axis)
    pairs = [(source, (source + steps) % count) for source in range(count)]
    return lax.ppermute(value, axis, pairs)


def shifted(array, axis, by):
    devices = lax.axis_size(axis)
    pairs = [(i, i + by) for i in range(devices) if 0 <= i + by < devices]
    return lax.ppermute(array, axis, pairs)


def unit_roots(rows, cols, period):
    row_ids = jnp.arange(rows, dtype=jnp.int32)[:, None]
    col_ids = jnp.arange(cols, dtype=jnp.int32)[None, :]
    angle = (row_ids * col_ids % period).astype(jnp.float32) * (-2.0 * math.pi / period)
    return (jnp.cos(angle), jnp.sin(angle))


def contract(form, left, right):
    return jnp.einsum(
        form, left, right, precision=lax.Precision.HIGH, preferred_element_type=jnp.float32
    )


def to_spectrum(parts, factor_a, factor_b):
    channels = parts.shape[0]
    inputs_count = parts.shape[1]
    half = factor_a // 2
    period = factor_a * factor_b
    fa_cos, fa_sin = unit_roots(factor_a, half, factor_a)
    first_table = jnp.stack([jnp.stack([fa_cos, -fa_sin]), jnp.stack([fa_sin, fa_cos])])[
        :, :inputs_count
    ]
    tw_cos, tw_sin = unit_roots(factor_a, factor_b, period)
    fb_cos, fb_sin = unit_roots(factor_b, factor_b, factor_b)
    second_table = jnp.stack([jnp.stack([fb_cos, fb_sin]), jnp.stack([-fb_sin, fb_cos])])
    shaped = parts.reshape(channels, inputs_count, half, factor_b)
    first = contract("qrca,nrab->nqcb", first_table, shaped)
    first_re = first[:, 0]
    first_im = first[:, 1]
    turned = jnp.stack(
        [first_re * tw_cos - first_im * tw_sin, first_re * tw_sin + first_im * tw_cos], 1
    )
    return contract("nqcb,qpbd->npcd", turned, second_table)


def from_spectrum(spectrum, factor_a, factor_b, scale):
    channels = spectrum.shape[0]
    half = factor_a // 2
    period = factor_a * factor_b
    fb_cos, fb_sin = unit_roots(factor_b, factor_b, factor_b)
    back_table = jnp.stack([jnp.stack([fb_cos, -fb_sin]), jnp.stack([fb_sin, fb_cos])])
    tw_cos, tw_sin = unit_roots(factor_a, factor_b, period)
    fa_cos, fa_sin = unit_roots(half, factor_a, factor_a)
    last_table = jnp.stack(
        [
            jnp.stack([fa_cos, fa_sin]) * (scale / period),
            jnp.stack([-fa_sin, fa_cos]) * (1.0 / period),
        ]
    )
    middle = contract("npcd,pqdb->nqcb", spectrum, back_table)
    middle_re = middle[:, 0]
    middle_im = middle[:, 1]
    turned = jnp.stack(
        [middle_re * tw_cos + middle_im * tw_sin, middle_im * tw_cos - middle_re * tw_sin], 1
    )
    result = contract("rqac,nqcb->nrab", last_table, turned)
    length = half * factor_b
    return (result[:, 0].reshape(channels, length), result[:, 1].reshape(channels, length))


def depthwise(extended, kernel):
    result = lax.conv_general_dilated(
        extended[None],
        kernel[:, None, :],
        (1,),
        "VALID",
        dimension_numbers=("NWC", "WIO", "NWC"),
        feature_group_count=extended.shape[1],
        preferred_element_type=jnp.float32,
    )
    return result[0]


def per_device(
    incoming, layer_input, pre_gate, mid_gate, long_gate, out_gate, long_filter, mid_filter
):
    sections = lax.axis_size("section")
    beta = (2.0 * sections) ** (-0.5)
    adjoint = passed_along(incoming[0], "section", -1).astype(jnp.float32)
    inputs = layer_input[0].astype(jnp.float32)
    tokens = inputs.shape[0]
    gate_pre = pre_gate[0].astype(jnp.float32)
    gate_mid = mid_gate[0].astype(jnp.float32)
    gate_long = long_gate[0].astype(jnp.float32)
    gate_out = out_gate[0].astype(jnp.float32)
    filter_taps = mid_filter[0]
    reach = filter_taps.shape[0] - 1
    seq_len = tokens * lax.axis_size("ctx")
    scale = float(seq_len) ** (-0.5)
    mixed_in = (inputs * gate_pre).astype(jnp.bfloat16)
    earlier = shifted(mixed_in[tokens - reach :], "ctx", 1)
    extended = jnp.concatenate([earlier, mixed_in], 0)
    branch = depthwise(extended, filter_taps[::-1])
    resid = inputs + beta * branch * gate_mid
    long_in = (resid * gate_long).astype(jnp.bfloat16)
    grad_z = (beta * adjoint * gate_out).astype(jnp.bfloat16)
    channel_z, channel_w = (
        lax.all_to_all(grad_z.T, "ctx", split_axis=0, concat_axis=1, tiled=True),
        lax.all_to_all(long_in.T, "ctx", split_axis=0, concat_axis=1, tiled=True),
    )
    factor_b = math.gcd(seq_len, 128)
    factor_a = 2 * seq_len // factor_b
    zspec = to_spectrum(channel_z[:, None], factor_a, factor_b)
    zspec_re = zspec[:, 0]
    zspec_im = zspec[:, 1]
    pair = to_spectrum(jnp.stack([channel_w, -long_filter[0]], 1), factor_a, factor_b)
    pair_re = pair[:, 0]
    pair_im = pair[:, 1]
    joint_re = zspec_re * pair_re + zspec_im * pair_im
    joint_im = zspec_im * pair_re - zspec_re * pair_im
    lag_grad, input_part = from_spectrum(
        jnp.stack([joint_re, joint_im], 1), factor_a, factor_b, scale
    )
    long_grad = lag_grad.astype(jnp.bfloat16)[None]
    returned = lax.all_to_all(
        input_part.astype(jnp.bfloat16), "ctx", split_axis=1, concat_axis=0, tiled=True
    ).T
    grad_u = adjoint + returned.astype(jnp.float32) * gate_long
    grad_b = (beta * grad_u * gate_mid).astype(jnp.bfloat16)
    later = shifted(grad_b[:reach], "ctx", -1)
    grad_act = depthwise(jnp.concatenate([grad_b, later], 0), filter_taps)
    input_grad = (grad_u + grad_act * gate_pre).astype(jnp.bfloat16)[None]
    tap_part = depthwise(extended, grad_b)[::-1]
    total_taps = lax.psum(tap_part, "ctx")
    columns = tap_part.shape[1] // lax.axis_size("ctx")
    own_taps = lax.dynamic_slice_in_dim(total_taps, lax.axis_index("ctx") * columns, columns, 1)
    mid_grad = (own_taps * scale).astype(jnp.bfloat16)[None]
    return (input_grad, long_grad, mid_grad)


def solution(mesh):
    placed = (
        P("section", "ctx", None),
        P("section", "ctx", None),
        P("section", "ctx", None),
        P("section", "ctx", None),
        P("section", "ctx", None),
        P("section", "ctx", None),
        P("section", "ctx", None),
        P("section", None, None),
    )
    return jax.shard_map(
        per_device,
        mesh=mesh,
        in_specs=placed,
        out_specs=(P("section", "ctx", None), P("section", "ctx", None), P("section", None, "ctx")),
        check_vma=False,
    )
```

profile of v0, /device:TPU:1, one launch (start us, length us, event | category | flops | bytes accessed | tf_op | source)
XLA Modules:
  0.0 466.3 jit_solution(479754405011131320)
XLA Ops:
  10.3 4.5 collective-permute-start.1
  16.0 10.8 %collective-permute-done.1 = bf16[127,4096]{1,0:T(8,128)(2,1)} collective-permute-done((bf16[127,4096]{1,0:T(8,128)(2,1)}, bf16[127,4096]{1,0:T(8,128)(2,1)}, u32[]{:S(2)}, u32[]{:S(2)}) %collective-permute-start.1) | collective-permute-done | bytes 1040416 | tf_op jit(solution)/shard_map/ppermute | solution.py:18
  28.4 27.4 %convolution_multiply_fusion = f32[1,128,4096]{2,0,1:T(1,128)S(1)} fusion(bf16[1,255,4096]{2,1,0:T(8,128)(2,1)S(1)} %maximum_bitcast_fusion.13, bf16[128,1,4096]{2,0,1:T(8,128)(2,1)S(1)} %bitcast.188), kind=kOutput, calls=%fused_computation.15 | convolution fusion | flops 134742016 | bytes 5234688 | tf_op jit(solution)/shard_map/conv_general_dilated | solution.py:82
  59.3 13.7 %all-to-all-start.1 = ((bf16[64,64,128]{2,1,0:T(8,128)(2,1)}), bf16[64,64,128]{2,1,0:T(8,128)(2,1)S(1)}, u32[]{:S(2)}, u32[]{:S(2)}) async-start(bf16[64,64,128]{2,1,0:T(8,128)(2,1)} %bitcast.35), calls=%async_computation.1 | async-start | bytes 2097152 | tf_op jit(solution)/shard_map/all_to_all | solution.py:119
  73.1 2.8 collective-permute-start
  75.9 22.4 %collective-permute-done = bf16[128,4096]{1,0:T(8,128)(2,1)S(1)} collective-permute-done((bf16[128,4096]{1,0:T(8,128)(2,1)}, bf16[128,4096]{1,0:T(8,128)(2,1)S(1)}, u32[]{:S(2)}, u32[]{:S(2)}) %collective-permute-start) | collective-permute-done | bytes 1048608 | tf_op jit(solution)/shard_map/ppermute | solution.py:12
  101.5 12.1 %all-to-all-start = ((bf16[64,64,128]{2,1,0:T(8,128)(2,1)}), bf16[64,64,128]{2,1,0:T(8,128)(2,1)}, u32[]{:S(2)}, u32[]{:S(2)}) async-start(bf16[64,64,128]{2,1,0:T(8,128)(2,1)} %bitcast.183), calls=%async_computation | async-start | bytes 2097152 | tf_op jit(solution)/shard_map/all_to_all | solution.py:118
  118.8 5.7 %convolution_bitcast_fusion.1 = f32[64,2,128,128]{2,3,1,0:T(8,128)} fusion(bf16[64,1,64,128]{3,2,1,0:T(8,128)(2,1)S(1)} %bitcast.184, bf16[64,1,64,128]{3,2,1,0:T(8,128)(2,1)S(1)} %bitcast.185, f32[1,2,128,64]{2,3,0,1:T(8,128)S(1)} %get-tuple-element.33, f32[1,2,128,64]{2,3,0,1:T(8,128)S(1)} %get-tuple-element.32), kind=kOutput, calls=%fused_computation.34 | convolution fusion | flops 1614839808 | bytes 10616832 | tf_op jit(solution)/shard_map/qrca,nrab->nqcb/dot_general | solution.py:29
  124.5 16.8 %all-to-all-done = bf16[64,64,128]{2,1,0:T(8,128)(2,1)} async-done(((bf16[64,64,128]{2,1,0:T(8,128)(2,1)}), bf16[64,64,128]{2,1,0:T(8,128)(2,1)}, u32[]{:S(2)}, u32[]{:S(2)}) %all-to-all-start) | async-done | bytes 1048608 | tf_op jit(solution)/shard_map/all_to_all | solution.py:118
  141.3 3.8 convolution_bitcast_fusion
  145.1 5.8 %multiply_subtract_fusion.3 = (f32[64,1,128,128]{2,3,1,0:T(8,128)}, f32[64,1,128,128]{2,3,1,0:T(8,128)}, f32[64,1,128,128]{2,3,1,0:T(8,128)S(1)}, f32[64,1,128,128]{2,3,1,0:T(8,128)}) fusion(f32[64,2,128,128]{2,3,1,0:T(8,128)S(1)} %convolution_bitcast_fusion, f32[128,128]{0,1:T(8,128)S(1)} %get-tuple-element.36, f32[128,128]{0,1:T(8,128)S(1)} %get-tuple-element.37, ...), kind=kLoop, calls=%fused_computation.24 | loop fusion | flops 12582912 | bytes 33685504 | tf_op jit(solution)/shard_map/sub | solution.py:51
  150.9 6.9 %fusion.20 = f32[64,2,128,128]{2,3,0,1:T(8,128)S(1)} fusion(f32[64,1,128,128]{2,3,1,0:T(8,128)} %get-tuple-element.17, f32[64,1,128,128]{2,3,1,0:T(8,128)} %get-tuple-element.16, f32[1,2,128,128]{2,3,0,1:T(8,128)S(1)} %get-tuple-element.23, f32[1,2,128,128]{2,3,0,1:T(8,128)S(1)} %get-tuple-element.28), kind=kOutput, calls=%fused_computation.33 | convolution fusion | flops 3223388160 | bytes 17039360 | tf_op jit(solution)/shard_map/nqcb,qpbd->npcd/dot_general | solution.py:29
  157.9 4.9 %fusion.19 = f32[64,2,128,128]{2,3,0,1:T(8,128)S(1)} fusion(f32[64,1,128,128]{2,3,1,0:T(8,128)S(1)} %get-tuple-element.26, f32[64,1,128,128]{2,3,1,0:T(8,128)S(1)} %copy-done.3, f32[1,2,128,128]{2,3,0,1:T(8,128)S(1)} %get-tuple-element.23, f32[1,2,128,128]{2,3,0,1:T(8,128)S(1)} %get-tuple-element.28), kind=kOutput, calls=%fused_computation.32 | convolution fusion | flops 3223388160 | bytes 17039360 | tf_op jit(solution)/shard_map/nqcb,qpbd->npcd/dot_general | solution.py:29
  164.7 5.0 %fusion.16 = f32[64,2,128,128]{2,3,1,0:T(8,128)S(1)} fusion(f32[64,1,128,128]{2,3,0,1:T(8,128)S(1)} %get-tuple-element.13, f32[64,1,128,128]{2,3,0,1:T(8,128)S(1)} %get-tuple-element.12, f32[1,2,128,128]{2,3,1,0:T(8,128)S(1)} %copy-done.20, f32[1,2,128,128]{2,3,1,0:T(8,128)S(1)} %copy-done.19), kind=kOutput, calls=%fused_computation.30 | convolution fusion | flops 3223388160 | bytes 17039360 | tf_op jit(solution)/shard_map/npcd,pqdb->nqcb/dot_general | solution.py:29
  171.6 4.6 fusion.33
  178.1 6.5 %all-to-all-start.2 = ((bf16[64,64,128]{2,0,1:T(8,128)(2,1)}), bf16[64,64,128]{2,0,1:T(8,128)(2,1)S(1)}, u32[]{:S(2)}, u32[]{:S(2)}) async-start(bf16[64,64,128]{2,0,1:T(8,128)(2,1)} %copy.65), calls=%async_computation.2 | async-start | bytes 2097152 | tf_op jit(solution)/shard_map/all_to_all | solution.py:135
  185.9 26.7 %all-to-all-done.2 = bf16[64,64,128]{2,0,1:T(8,128)(2,1)S(1)} async-done(((bf16[64,64,128]{2,0,1:T(8,128)(2,1)}), bf16[64,64,128]{2,0,1:T(8,128)(2,1)S(1)}, u32[]{:S(2)}, u32[]{:S(2)}) %all-to-all-start.2) | async-done | bytes 1048608 | tf_op jit(solution)/shard_map/all_to_all | solution.py:135
  216.1 3.9 fusion.23
  220.0 3.3 collective-permute-start.2
  223.3 28.8 %fusion.13 = f32[1,128,4096]{2,0,1:T(1,128)S(1)} fusion(bf16[1,255,4096]{2,1,0:T(8,128)(2,1)S(1)} %copy-done.12, bf16[128,1,4096]{2,0,1:T(8,128)(2,1)} %bitcast.72), kind=kOutput, calls=%fused_computation.27 | convolution fusion | flops 134217728 | bytes 5234688 | tf_op jit(solution)/shard_map/conv_general_dilated | solution.py:82
  252.1 3.0 copy.131
  255.1 16.6 %rev.7 = f32[128,4096]{1,0:T(8,128)} reverse(f32[128,4096]{1,0:T(8,128)} %bitcast.182), dimensions={0} | reverse | bytes 4194304 | tf_op jit(solution)/shard_map/rev | solution.py:143
  273.3 30.1 %fusion.11 = f32[1,128,4096]{2,0,1:T(1,128)S(1)} fusion(bf16[1,255,4096]{2,1,0:T(8,128)(2,1)S(1)} %maximum_bitcast_fusion.16, bf16[128,1,4096]{2,0,1:T(8,128)(2,1)S(1)} %bitcast.187), kind=kOutput, calls=%fused_computation.25 | convolution fusion | flops 134217728 | bytes 5234688 | tf_op jit(solution)/shard_map/conv_general_dilated | solution.py:82
  306.3 151.3 %all-reduce.2.cloned.1.call-done = f32[128,4096]{1,0:T(8,128)} async-done(((f32[128,4096]{1,0:T(8,128)}), f32[128,4096]{1,0:T(8,128)}) %all-reduce.2.cloned.1.call-update) | async-done | bytes 2097168 | tf_op jit(solution)/shard_map/psum | solution.py:144
  (78 shorter events, 34.1 us)
Async XLA Ops:
  7.2 7.6 %copy-start.13 = (bf16[1,128,4096]{2,1,0:T(8,128)(2,1)S(1)}, bf16[1,128,4096]{2,1,0:T(8,128)(2,1)}, u32[]{:S(2)}) copy-start(bf16[1,128,4096]{2,1,0:T(8,128)(2,1)} %param.15) | copy-start | bytes 3145732
  10.3 16.5 %collective-permute-start.1 = (bf16[127,4096]{1,0:T(8,128)(2,1)}, bf16[127,4096]{1,0:T(8,128)(2,1)}, u32[]{:S(2)}, u32[]{:S(2)}) collective-permute-start(bf16[127,4096]{1,0:T(8,128)(2,1)} %slice.67), channel_id=1, source_target_pairs={{0,1},{1,2},{2,3},{3,4},{4,5},{5,6},{6,7},{7,8},{8,9},{9,10},{10,1... | collective-permute-start | bytes 3121160 | tf_op jit(solution)/shard_map/ppermute | solution.py:18
  28.4 27.5 %copy-start.11 = (bf16[1,255,4096]{2,1,0:T(8,128)(2,1)}, bf16[1,255,4096]{2,1,0:T(8,128)(2,1)S(1)}, u32[]{:S(2)}) copy-start(bf16[1,255,4096]{2,1,0:T(8,128)(2,1)S(1)} %maximum_bitcast_fusion.13) | copy-start | bytes 6266884
  28.4 27.5 %copy-start.6 = (bf16[1,128,4096]{2,1,0:T(8,128)(2,1)S(1)}, bf16[1,128,4096]{2,1,0:T(8,128)(2,1)}, u32[]{:S(2)}) copy-start(bf16[1,128,4096]{2,1,0:T(8,128)(2,1)} %param.12) | copy-start | bytes 3145732
  28.4 27.5 %copy-start.8 = (bf16[1,128,4096]{2,1,0:T(8,128)(2,1)S(1)}, bf16[1,128,4096]{2,1,0:T(8,128)(2,1)}, u32[]{:S(2)}) copy-start(bf16[1,128,4096]{2,1,0:T(8,128)(2,1)} %param.9) | copy-start | bytes 3145732
  28.4 27.5 %copy-start.9 = (bf16[1,128,4096]{2,1,0:T(8,128)(2,1)S(1)}, bf16[1,128,4096]{2,1,0:T(8,128)(2,1)}, u32[]{:S(2)}) copy-start(bf16[1,128,4096]{2,1,0:T(8,128)(2,1)} %param.11) | copy-start | bytes 3145732
  59.3 42.2 %all-to-all-start.1 = ((bf16[64,64,128]{2,1,0:T(8,128)(2,1)}), bf16[64,64,128]{2,1,0:T(8,128)(2,1)S(1)}, u32[]{:S(2)}, u32[]{:S(2)}) async-start(bf16[64,64,128]{2,1,0:T(8,128)(2,1)} %bitcast.35), calls=%async_computation.1 | async-start | bytes 2097152 | tf_op jit(solution)/shard_map/all_to_all | solution.py:119
  73.1 25.2 %collective-permute-start = (bf16[128,4096]{1,0:T(8,128)(2,1)}, bf16[128,4096]{1,0:T(8,128)(2,1)S(1)}, u32[]{:S(2)}, u32[]{:S(2)}) collective-permute-start(bf16[128,4096]{1,0:T(8,128)(2,1)} %bitcast.189), channel_id=1, source_target_pairs={{0,192},{64,0},{128,64},{192,128},{1,193},{65,1},{129,65},{193,129... | collective-permute-start | bytes 3145736 | tf_op jit(solution)/shard_map/ppermute | solution.py:12
  98.3 117.8 %copy-start.4 = (bf16[128,4096]{1,0:T(8,128)(2,1)}, bf16[128,4096]{1,0:T(8,128)(2,1)S(1)}, u32[]{:S(2)}) copy-start(bf16[128,4096]{1,0:T(8,128)(2,1)S(1)} %collective-permute-done) | copy-start | bytes 3145732
  101.5 39.8 %all-to-all-start = ((bf16[64,64,128]{2,1,0:T(8,128)(2,1)}), bf16[64,64,128]{2,1,0:T(8,128)(2,1)}, u32[]{:S(2)}, u32[]{:S(2)}) async-start(bf16[64,64,128]{2,1,0:T(8,128)(2,1)} %bitcast.183), calls=%async_computation | async-start | bytes 2097152 | tf_op jit(solution)/shard_map/all_to_all | solution.py:118
  116.7 2.1 copy-start.15
  116.7 2.1 copy-start.16
  141.3 3.8 copy-start
  150.9 7.0 %copy-start.3 = (f32[64,1,128,128]{2,3,1,0:T(8,128)S(1)}, f32[64,1,128,128]{2,3,1,0:T(8,128)}, u32[]{:S(2)}) copy-start(f32[64,1,128,128]{2,3,1,0:T(8,128)} %get-tuple-element.27) | copy-start | bytes 12582916
  169.7 1.9 copy-start.17
  178.1 34.5 %all-to-all-start.2 = ((bf16[64,64,128]{2,0,1:T(8,128)(2,1)}), bf16[64,64,128]{2,0,1:T(8,128)(2,1)S(1)}, u32[]{:S(2)}, u32[]{:S(2)}) async-start(bf16[64,64,128]{2,0,1:T(8,128)(2,1)} %copy.65), calls=%async_computation.2 | async-start | bytes 2097152 | tf_op jit(solution)/shard_map/all_to_all | solution.py:135
  184.6 273.0 %all-reduce.2.cloned.1.call-start = ((), (), s32[]{:S(2)}) async-start(), calls=%async_computation.3 | async-start | bytes 4194304 | tf_op jit(solution)/shard_map/psum | solution.py:144
  216.1 35.9 %copy-start.1 = (f32[4096,128]{0,1:T(8,128)}, f32[4096,128]{0,1:T(8,128)S(1)}, u32[]{:S(2)}) copy-start(f32[4096,128]{0,1:T(8,128)S(1)} %copy.66) | copy-start | bytes 6291460
  216.1 7.2 %copy-start.12 = (bf16[1,255,4096]{2,1,0:T(8,128)(2,1)S(1)}, bf16[1,255,4096]{2,1,0:T(8,128)(2,1)}, u32[]{:S(2)}) copy-start(bf16[1,255,4096]{2,1,0:T(8,128)(2,1)} %copy-done.11) | copy-start | bytes 6266884
  220.0 51.7 %collective-permute-start.2 = (bf16[127,4096]{1,0:T(8,128)(2,1)}, bf16[127,4096]{1,0:T(8,128)(2,1)S(1)}, u32[]{:S(2)}, u32[]{:S(2)}) collective-permute-start(bf16[127,4096]{1,0:T(8,128)(2,1)} %bitcast.180), channel_id=1, source_target_pairs={{1,0},{2,1},{3,2},{4,3},{5,4},{6,5},{7,6},{8,7},{9,8},{10,9},{11,1... | collective-permute-start | bytes 3121160 | tf_op jit(solution)/shard_map/ppermute | solution.py:18
  273.3 30.2 %copy-start.2 = (f32[4096,128]{0,1:T(8,128)S(1)}, f32[4096,128]{0,1:T(8,128)}, u32[]{:S(2)}) copy-start(f32[4096,128]{0,1:T(8,128)} %copy-done.1) | copy-start | bytes 6291460
  273.3 30.2 %copy-start.5 = (bf16[128,4096]{1,0:T(8,128)(2,1)S(1)}, bf16[128,4096]{1,0:T(8,128)(2,1)}, u32[]{:S(2)}) copy-start(bf16[128,4096]{1,0:T(8,128)(2,1)} %copy-done.4) | copy-start | bytes 3145732
  273.3 30.2 %copy-start.7 = (bf16[1,128,4096]{2,1,0:T(8,128)(2,1)S(1)}, bf16[1,128,4096]{2,1,0:T(8,128)(2,1)}, u32[]{:S(2)}) copy-start(bf16[1,128,4096]{2,1,0:T(8,128)(2,1)} %param.12) | copy-start | bytes 3145732
  273.3 30.2 %copy-start.10 = (bf16[1,128,4096]{2,1,0:T(8,128)(2,1)S(1)}, bf16[1,128,4096]{2,1,0:T(8,128)(2,1)}, u32[]{:S(2)}) copy-start(bf16[1,128,4096]{2,1,0:T(8,128)(2,1)} %param.10) | copy-start | bytes 3145732
  (4 other events, 7.2 us)
Sparse Core Ops, SparseCore 0:
  271.9 185.6 all-reduce.1
where the time goes:
time: 474 us; the launch traced here: 466 us
  waiting for transfers between devices  228 us (48%)
  matrix products  117 us (25%)
  starting transfers between devices  42.9 us (9%)
  other arithmetic  31.9 us (7%)
  local copies, waits for them, and re-layouts  31.5 us (7%)
  between operations  14.8 us (3%)
    psum x1, waiting for transfers between devices, per_device(): total_taps = lax.psum(tap_part, 'ctx')  151 us
    conv_general_dilated x3, matrix products, depthwise(): lax.conv_general_dilated(extended[None], kernel[:, None, :], (1,), 'VALID...  86.3 us
    dot_general x6, matrix products, contract(): jnp.einsum(form, left, right, precision=lax.Precision.HIGH, preferred_ele...  31 us
    all_to_all x1, waiting for transfers between devices, per_device(): lax.all_to_all(input_part.astype(jnp.bfloat16), 'ctx', split_axis=1, conc...  26.7 us
    ppermute x1, waiting for transfers between devices, passed_along(): return lax.ppermute(value, axis, pairs)  22.4 us
    all_to_all x1, waiting for transfers between devices, per_device(): lax.all_to_all(grad_z.T, 'ctx', split_axis=0, concat_axis=1, tiled=True)  16.8 us
    rev x1, local copies, waits for them, and re-layouts, per_device(): tap_part = depthwise(extended, grad_b)[::-1]  16.6 us
    all_to_all x1, starting transfers between devices, per_device(): lax.all_to_all(long_in.T, 'ctx', split_axis=0, concat_axis=1, tiled=True)  13.7 us
  transfers between devices with their start and end apart: 7, of which 5 were waited for; matrix products, arithmetic and copies ran while one was open for 21% of the time, Pallas kernels for 0%

commit v1 on v0

--- a/solution.py
+++ b/solution.py
@@ -141,9 +141,7 @@
     grad_act = depthwise(jnp.concatenate([grad_b, later], 0), filter_taps)
     input_grad = (grad_u + grad_act * gate_pre).astype(jnp.bfloat16)[None]
     tap_part = depthwise(extended, grad_b)[::-1]
-    total_taps = lax.psum(tap_part, "ctx")
-    columns = tap_part.shape[1] // lax.axis_size("ctx")
-    own_taps = lax.dynamic_slice_in_dim(total_taps, lax.axis_index("ctx") * columns, columns, 1)
+    own_taps = lax.psum_scatter(tap_part, "ctx", scatter_dimension=1, tiled=True)
     mid_grad = (own_taps * scale).astype(jnp.bfloat16)[None]
     return (input_grad, long_grad, mid_grad)
 

time: 474 us -> 424 us (0.89)
  the two profiles are of different devices: /device:TPU:1 before, /device:TPU:8 now
where the time goes in v1:
time: 424 us; the launch traced here: 417 us
  waiting for transfers between devices  177 us (42%)
  matrix products  117 us (28%)
  starting transfers between devices  45.9 us (11%)
  local copies, waits for them, and re-layouts  31.1 us (7%)
  other arithmetic  30.8 us (7%)
  between operations  14.8 us (3%)
    unnamed x2, waiting for transfers between devices  106 us
    conv_general_dilated x3, matrix products, depthwise(): lax.conv_general_dilated(extended[None], kernel[:, None, :], (1,), 'VALID...  86.3 us
    dot_general x6, matrix products, contract(): jnp.einsum(form, left, right, precision=lax.Precision.HIGH, preferred_ele...  31 us
    all_to_all x1, waiting for transfers between devices, per_device(): lax.all_to_all(input_part.astype(jnp.bfloat16), 'ctx', split_axis=1, conc...  27.6 us
    ppermute x1, waiting for transfers between devices, passed_along(): return lax.ppermute(value, axis, pairs)  24.9 us
    all_to_all x1, starting transfers between devices, per_device(): lax.all_to_all(long_in.T, 'ctx', split_axis=0, concat_axis=1, tiled=True)  24.9 us
    all_to_all x1, waiting for transfers between devices, per_device(): lax.all_to_all(grad_z.T, 'ctx', split_axis=0, concat_axis=1, tiled=True)  17.8 us
    rev x1, local copies, waits for them, and re-layouts, per_device(): tap_part = depthwise(extended, grad_b)[::-1]  13.6 us
  transfers between devices with their start and end apart: 7, of which 6 were waited for; matrix products, arithmetic and copies ran while one was open for 24% of the time, Pallas kernels for 0%

profile of v1, /device:TPU:8, one launch (start us, length us, event | category | flops | bytes accessed | tf_op | source)
XLA Modules:
  0.0 416.9 jit_solution(13020324167257536378)
XLA Ops:
  10.3 2.7 collective-permute-start.1
  16.2 27.4 %convolution_multiply_fusion = f32[1,128,4096]{2,0,1:T(1,128)S(1)} fusion(bf16[1,255,4096]{2,1,0:T(8,128)(2,1)S(1)} %maximum_bitcast_fusion.13, bf16[128,1,4096]{2,0,1:T(8,128)(2,1)S(1)} %bitcast.191), kind=kOutput, calls=%fused_computation.15 | convolution fusion | flops 134742016 | bytes 5234688 | tf_op jit(solution)/shard_map/conv_general_dilated | solution.py:82
  43.7 2.1 fusion.34
  47.1 24.9 %all-to-all-start.1 = ((bf16[64,64,128]{2,1,0:T(8,128)(2,1)}), bf16[64,64,128]{2,1,0:T(8,128)(2,1)S(1)}, u32[]{:S(2)}, u32[]{:S(2)}) async-start(bf16[64,64,128]{2,1,0:T(8,128)(2,1)} %bitcast.35), calls=%async_computation.1 | async-start | bytes 2097152 | tf_op jit(solution)/shard_map/all_to_all | solution.py:119
  72.5 24.9 %collective-permute-done = bf16[128,4096]{1,0:T(8,128)(2,1)S(1)} collective-permute-done((bf16[128,4096]{1,0:T(8,128)(2,1)}, bf16[128,4096]{1,0:T(8,128)(2,1)S(1)}, u32[]{:S(2)}, u32[]{:S(2)}) %collective-permute-start) | collective-permute-done | bytes 1048608 | tf_op jit(solution)/shard_map/ppermute | solution.py:12
  100.8 10.9 %all-to-all-start = ((bf16[64,64,128]{2,1,0:T(8,128)(2,1)}), bf16[64,64,128]{2,1,0:T(8,128)(2,1)}, u32[]{:S(2)}, u32[]{:S(2)}) async-start(bf16[64,64,128]{2,1,0:T(8,128)(2,1)} %bitcast.186), calls=%async_computation | async-start | bytes 2097152 | tf_op jit(solution)/shard_map/all_to_all | solution.py:118
  116.9 5.7 %convolution_bitcast_fusion.1 = f32[64,2,128,128]{2,3,1,0:T(8,128)} fusion(bf16[64,1,64,128]{3,2,1,0:T(8,128)(2,1)S(1)} %bitcast.187, bf16[64,1,64,128]{3,2,1,0:T(8,128)(2,1)S(1)} %bitcast.188, f32[1,2,128,64]{2,3,0,1:T(8,128)S(1)} %get-tuple-element.33, f32[1,2,128,64]{2,3,0,1:T(8,128)S(1)} %get-tuple-element.32), kind=kOutput, calls=%fused_computation.34 | convolution fusion | flops 1614839808 | bytes 10616832 | tf_op jit(solution)/shard_map/qrca,nrab->nqcb/dot_general | solution.py:29
  122.6 17.8 %all-to-all-done = bf16[64,64,128]{2,1,0:T(8,128)(2,1)} async-done(((bf16[64,64,128]{2,1,0:T(8,128)(2,1)}), bf16[64,64,128]{2,1,0:T(8,128)(2,1)}, u32[]{:S(2)}, u32[]{:S(2)}) %all-to-all-start) | async-done | bytes 1048608 | tf_op jit(solution)/shard_map/all_to_all | solution.py:118
  140.4 3.8 convolution_bitcast_fusion
  144.3 5.8 %multiply_subtract_fusion.3 = (f32[64,1,128,128]{2,3,1,0:T(8,128)}, f32[64,1,128,128]{2,3,1,0:T(8,128)}, f32[64,1,128,128]{2,3,1,0:T(8,128)S(1)}, f32[64,1,128,128]{2,3,1,0:T(8,128)}) fusion(f32[64,2,128,128]{2,3,1,0:T(8,128)S(1)} %convolution_bitcast_fusion, f32[128,128]{0,1:T(8,128)S(1)} %get-tuple-element.36, f32[128,128]{0,1:T(8,128)S(1)} %get-tuple-element.37, ...), kind=kLoop, calls=%fused_computation.24 | loop fusion | flops 12582912 | bytes 33685504 | tf_op jit(solution)/shard_map/sub | solution.py:51
  150.1 6.9 %fusion.20 = f32[64,2,128,128]{2,3,0,1:T(8,128)S(1)} fusion(f32[64,1,128,128]{2,3,1,0:T(8,128)} %get-tuple-element.17, f32[64,1,128,128]{2,3,1,0:T(8,128)} %get-tuple-element.16, f32[1,2,128,128]{2,3,0,1:T(8,128)S(1)} %get-tuple-element.23, f32[1,2,128,128]{2,3,0,1:T(8,128)S(1)} %get-tuple-element.28), kind=kOutput, calls=%fused_computation.33 | convolution fusion | flops 3223388160 | bytes 17039360 | tf_op jit(solution)/shard_map/nqcb,qpbd->npcd/dot_general | solution.py:29
  157.0 4.9 %fusion.19 = f32[64,2,128,128]{2,3,0,1:T(8,128)S(1)} fusion(f32[64,1,128,128]{2,3,1,0:T(8,128)S(1)} %get-tuple-element.26, f32[64,1,128,128]{2,3,1,0:T(8,128)S(1)} %copy-done.3, f32[1,2,128,128]{2,3,0,1:T(8,128)S(1)} %get-tuple-element.23, f32[1,2,128,128]{2,3,0,1:T(8,128)S(1)} %get-tuple-element.28), kind=kOutput, calls=%fused_computation.32 | convolution fusion | flops 3223388160 | bytes 17039360 | tf_op jit(solution)/shard_map/nqcb,qpbd->npcd/dot_general | solution.py:29
  163.8 5.0 %fusion.16 = f32[64,2,128,128]{2,3,1,0:T(8,128)S(1)} fusion(f32[64,1,128,128]{2,3,0,1:T(8,128)S(1)} %get-tuple-element.13, f32[64,1,128,128]{2,3,0,1:T(8,128)S(1)} %get-tuple-element.12, f32[1,2,128,128]{2,3,1,0:T(8,128)S(1)} %copy-done.20, f32[1,2,128,128]{2,3,1,0:T(8,128)S(1)} %copy-done.19), kind=kOutput, calls=%fused_computation.30 | convolution fusion | flops 3223388160 | bytes 17039360 | tf_op jit(solution)/shard_map/npcd,pqdb->nqcb/dot_general | solution.py:29
  170.8 4.7 %fusion.33 = bf16[64,2,64,128]{3,2,1,0:T(8,128)(2,1)S(1)} fusion(f32[64,1,128,128]{2,3,1,0:T(8,128)S(1)} %get-tuple-element.15, f32[64,1,128,128]{2,3,1,0:T(8,128)S(1)} %get-tuple-element.14, f32[1,2,64,128]{3,2,1,0:T(8,128)S(1)} %copy-done.18, f32[1,2,64,128]{3,2,1,0:T(8,128)S(1)} %copy-done.17), kind=kOutput, calls=%fused_computation.60 | convolution fusion | flops 1613791232 | bytes 10616832 | tf_op jit(solution)/shard_map/rqac,nqcb->nrab/dot_general | solution.py:29
  177.3 5.6 %all-to-all-start.2 = ((bf16[64,64,128]{2,0,1:T(8,128)(2,1)}), bf16[64,64,128]{2,0,1:T(8,128)(2,1)S(1)}, u32[]{:S(2)}, u32[]{:S(2)}) async-start(bf16[64,64,128]{2,0,1:T(8,128)(2,1)} %copy.65), calls=%async_computation.2 | async-start | bytes 2097152 | tf_op jit(solution)/shard_map/all_to_all | solution.py:135
  184.2 27.6 %all-to-all-done.2 = bf16[64,64,128]{2,0,1:T(8,128)(2,1)S(1)} async-done(((bf16[64,64,128]{2,0,1:T(8,128)(2,1)}), bf16[64,64,128]{2,0,1:T(8,128)(2,1)S(1)}, u32[]{:S(2)}, u32[]{:S(2)}) %all-to-all-start.2) | async-done | bytes 1048608 | tf_op jit(solution)/shard_map/all_to_all | solution.py:135
  213.3 1.9 copy.66
  215.3 3.9 fusion.23
  220.5 28.8 %fusion.13 = f32[1,128,4096]{2,0,1:T(1,128)S(1)} fusion(bf16[1,255,4096]{2,1,0:T(8,128)(2,1)S(1)} %copy-done.12, bf16[128,1,4096]{2,0,1:T(8,128)(2,1)} %bitcast.72), kind=kOutput, calls=%fused_computation.27 | convolution fusion | flops 134217728 | bytes 5234688 | tf_op jit(solution)/shard_map/conv_general_dilated | solution.py:82
  249.2 3.0 copy.133
  252.2 13.6 %rev.7 = f32[128,4096]{1,0:T(8,128)S(1)} reverse(f32[128,4096]{1,0:T(8,128)} %bitcast.185), dimensions={0} | reverse | bytes 4194304 | tf_op jit(solution)/shard_map/rev | solution.py:143
  269.3 30.1 %fusion.11 = f32[1,128,4096]{2,0,1:T(1,128)S(1)} fusion(bf16[1,255,4096]{2,1,0:T(8,128)(2,1)S(1)} %maximum_bitcast_fusion.16, bf16[128,1,4096]{2,0,1:T(8,128)(2,1)S(1)} %bitcast.190), kind=kOutput, calls=%fused_computation.25 | convolution fusion | flops 134217728 | bytes 5234688 | tf_op jit(solution)/shard_map/conv_general_dilated | solution.py:82
  299.4 2.8 fusion.35
  302.3 106.1 %reduce-scatter.4.cloned.1.call-done = f32[64,128]{1,0:T(8,128)} async-done(((f32[4096,128]{1,0:T(8,128)}), f32[64,128]{1,0:T(8,128)}) %reduce-scatter.4.cloned.1.call-update) | async-done | bytes 32784
  (80 shorter events, 31.4 us)
Async XLA Ops:
  7.2 5.9 %copy-start.13 = (bf16[1,128,4096]{2,1,0:T(8,128)(2,1)S(1)}, bf16[1,128,4096]{2,1,0:T(8,128)(2,1)}, u32[]{:S(2)}) copy-start(bf16[1,128,4096]{2,1,0:T(8,128)(2,1)} %param.15) | copy-start | bytes 3145732
  10.3 4.3 %collective-permute-start.1 = (bf16[127,4096]{1,0:T(8,128)(2,1)}, bf16[127,4096]{1,0:T(8,128)(2,1)}, u32[]{:S(2)}, u32[]{:S(2)}) collective-permute-start(bf16[127,4096]{1,0:T(8,128)(2,1)} %slice.67), channel_id=1, source_target_pairs={{0,1},{1,2},{2,3},{3,4},{4,5},{5,6},{6,7},{7,8},{8,9},{9,10},{10,1... | collective-permute-start | bytes 3121160 | tf_op jit(solution)/shard_map/ppermute | solution.py:18
  16.2 27.5 %copy-start.11 = (bf16[1,255,4096]{2,1,0:T(8,128)(2,1)}, bf16[1,255,4096]{2,1,0:T(8,128)(2,1)S(1)}, u32[]{:S(2)}) copy-start(bf16[1,255,4096]{2,1,0:T(8,128)(2,1)S(1)} %maximum_bitcast_fusion.13) | copy-start | bytes 6266884
  16.2 27.5 %copy-start.6 = (bf16[1,128,4096]{2,1,0:T(8,128)(2,1)S(1)}, bf16[1,128,4096]{2,1,0:T(8,128)(2,1)}, u32[]{:S(2)}) copy-start(bf16[1,128,4096]{2,1,0:T(8,128)(2,1)} %param.12) | copy-start | bytes 3145732
  16.2 27.5 %copy-start.8 = (bf16[1,128,4096]{2,1,0:T(8,128)(2,1)S(1)}, bf16[1,128,4096]{2,1,0:T(8,128)(2,1)}, u32[]{:S(2)}) copy-start(bf16[1,128,4096]{2,1,0:T(8,128)(2,1)} %param.9) | copy-start | bytes 3145732
  16.2 27.5 %copy-start.9 = (bf16[1,128,4096]{2,1,0:T(8,128)(2,1)S(1)}, bf16[1,128,4096]{2,1,0:T(8,128)(2,1)}, u32[]{:S(2)}) copy-start(bf16[1,128,4096]{2,1,0:T(8,128)(2,1)} %param.11) | copy-start | bytes 3145732
  47.1 53.8 %all-to-all-start.1 = ((bf16[64,64,128]{2,1,0:T(8,128)(2,1)}), bf16[64,64,128]{2,1,0:T(8,128)(2,1)S(1)}, u32[]{:S(2)}, u32[]{:S(2)}) async-start(bf16[64,64,128]{2,1,0:T(8,128)(2,1)} %bitcast.35), calls=%async_computation.1 | async-start | bytes 2097152 | tf_op jit(solution)/shard_map/all_to_all | solution.py:119
  71.9 25.4 %collective-permute-start = (bf16[128,4096]{1,0:T(8,128)(2,1)}, bf16[128,4096]{1,0:T(8,128)(2,1)S(1)}, u32[]{:S(2)}, u32[]{:S(2)}) collective-permute-start(bf16[128,4096]{1,0:T(8,128)(2,1)} %bitcast.193), channel_id=1, source_target_pairs={{0,192},{64,0},{128,64},{192,128},{1,193},{65,1},{129,65},{193,129... | collective-permute-start | bytes 3145736 | tf_op jit(solution)/shard_map/ppermute | solution.py:12
  97.4 117.9 %copy-start.4 = (bf16[128,4096]{1,0:T(8,128)(2,1)}, bf16[128,4096]{1,0:T(8,128)(2,1)S(1)}, u32[]{:S(2)}) copy-start(bf16[128,4096]{1,0:T(8,128)(2,1)S(1)} %collective-permute-done) | copy-start | bytes 3145732
  100.8 39.6 %all-to-all-start = ((bf16[64,64,128]{2,1,0:T(8,128)(2,1)}), bf16[64,64,128]{2,1,0:T(8,128)(2,1)}, u32[]{:S(2)}, u32[]{:S(2)}) async-start(bf16[64,64,128]{2,1,0:T(8,128)(2,1)} %bitcast.186), calls=%async_computation | async-start | bytes 2097152 | tf_op jit(solution)/shard_map/all_to_all | solution.py:118
  114.8 2.1 copy-start.15
  114.8 2.1 copy-start.16
  140.4 3.8 copy-start
  150.1 7.0 %copy-start.3 = (f32[64,1,128,128]{2,3,1,0:T(8,128)S(1)}, f32[64,1,128,128]{2,3,1,0:T(8,128)}, u32[]{:S(2)}) copy-start(f32[64,1,128,128]{2,3,1,0:T(8,128)} %get-tuple-element.27) | copy-start | bytes 12582916
  168.8 1.9 copy-start.17
  177.3 34.5 %all-to-all-start.2 = ((bf16[64,64,128]{2,0,1:T(8,128)(2,1)}), bf16[64,64,128]{2,0,1:T(8,128)(2,1)S(1)}, u32[]{:S(2)}, u32[]{:S(2)}) async-start(bf16[64,64,128]{2,0,1:T(8,128)(2,1)} %copy.65), calls=%async_computation.2 | async-start | bytes 2097152 | tf_op jit(solution)/shard_map/all_to_all | solution.py:135
  182.8 225.5 %reduce-scatter.4.cloned.1.call-start = ((), (), s32[]{:S(2)}) async-start(), calls=%async_computation.4 | async-start | bytes 2129920
  215.3 34.0 %copy-start.1 = (f32[4096,128]{0,1:T(8,128)}, f32[4096,128]{0,1:T(8,128)S(1)}, u32[]{:S(2)}) copy-start(f32[4096,128]{0,1:T(8,128)S(1)} %copy.66) | copy-start | bytes 6291460
  215.3 5.2 %copy-start.12 = (bf16[1,255,4096]{2,1,0:T(8,128)(2,1)S(1)}, bf16[1,255,4096]{2,1,0:T(8,128)(2,1)}, u32[]{:S(2)}) copy-start(bf16[1,255,4096]{2,1,0:T(8,128)(2,1)} %copy-done.11) | copy-start | bytes 6266884
  219.2 48.6 %collective-permute-start.2 = (bf16[127,4096]{1,0:T(8,128)(2,1)}, bf16[127,4096]{1,0:T(8,128)(2,1)S(1)}, u32[]{:S(2)}, u32[]{:S(2)}) collective-permute-start(bf16[127,4096]{1,0:T(8,128)(2,1)} %bitcast.182), channel_id=1, source_target_pairs={{1,0},{2,1},{3,2},{4,3},{5,4},{6,5},{7,6},{8,7},{9,8},{10,9},{11,1... | collective-permute-start | bytes 3121160 | tf_op jit(solution)/shard_map/ppermute | solution.py:18
  269.2 30.2 %copy-start.2 = (f32[4096,128]{0,1:T(8,128)S(1)}, f32[4096,128]{0,1:T(8,128)}, u32[]{:S(2)}) copy-start(f32[4096,128]{0,1:T(8,128)} %copy-done.1) | copy-start | bytes 6291460
  269.2 30.2 %copy-start.5 = (bf16[128,4096]{1,0:T(8,128)(2,1)S(1)}, bf16[128,4096]{1,0:T(8,128)(2,1)}, u32[]{:S(2)}) copy-start(bf16[128,4096]{1,0:T(8,128)(2,1)} %copy-done.4) | copy-start | bytes 3145732
  269.3 30.2 %copy-start.7 = (bf16[1,128,4096]{2,1,0:T(8,128)(2,1)S(1)}, bf16[1,128,4096]{2,1,0:T(8,128)(2,1)}, u32[]{:S(2)}) copy-start(bf16[1,128,4096]{2,1,0:T(8,128)(2,1)} %param.12) | copy-start | bytes 3145732
  269.3 30.2 %copy-start.10 = (bf16[1,128,4096]{2,1,0:T(8,128)(2,1)S(1)}, bf16[1,128,4096]{2,1,0:T(8,128)(2,1)}, u32[]{:S(2)}) copy-start(bf16[1,128,4096]{2,1,0:T(8,128)(2,1)} %param.10) | copy-start | bytes 3145732
  (4 other events, 7.1 us)
Sparse Core Ops, SparseCore 0:
  267.8 140.4 reduce-scatter.3

commit v2 on v1

--- a/solution.py
+++ b/solution.py
@@ -1,9 +1,77 @@
+import functools
 import math
 
 import jax
 import jax.numpy as jnp
 from jax import lax
+from jax.experimental import pallas as pl
+from jax.experimental.pallas import tpu as pltpu
 from jax.sharding import PartitionSpec as P
+
+MESH_IDS = pl.DeviceIdType.MESH
+
+
+def tap_exchange_kernel(n, scale, x_ref, o_ref, recv, send_sems, recv_sems):
+    me = lax.axis_index("ctx")
+    sec = lax.axis_index("section")
+    barrier = pltpu.get_barrier_semaphore()
+
+    def greet(k, carry):
+        peer = lax.rem(me + k, n)
+        pl.semaphore_signal(barrier, inc=1, device_id=(sec, peer), device_id_type=MESH_IDS)
+        return carry
+
+    lax.fori_loop(1, n, greet, 0)
+    pl.semaphore_wait(barrier, n - 1)
+
+    def copy_to(peer):
+        return pltpu.make_async_remote_copy(
+            src_ref=x_ref.at[peer],
+            dst_ref=recv.at[me],
+            send_sem=send_sems.at[peer],
+            recv_sem=recv_sems.at[me],
+            device_id=(sec, peer),
+            device_id_type=MESH_IDS,
+        )
+
+    def start(k, carry):
+        copy_to(lax.rem(me + k, n)).start()
+        return carry
+
+    lax.fori_loop(1, n, start, 0)
+    recv[me] = x_ref[me]
+
+    def wait_from(k, carry):
+        src = lax.rem(me + n - k, n)
+        pltpu.make_async_remote_copy(
+            src_ref=x_ref.at[src],
+            dst_ref=recv.at[src],
+            send_sem=send_sems.at[src],
+            recv_sem=recv_sems.at[src],
+            device_id=(sec, src),
+            device_id_type=MESH_IDS,
+        ).wait_recv()
+        copy_to(lax.rem(me + k, n)).wait_send()
+        return carry
+
+    lax.fori_loop(1, n, wait_from, 0)
+    o_ref[...] = (jnp.sum(recv[...], axis=0) * scale).astype(o_ref.dtype)
+
+
+def tap_exchange(parts, scale):
+    n, taps, width = parts.shape
+    return pl.pallas_call(
+        functools.partial(tap_exchange_kernel, n, scale),
+        out_shape=jax.ShapeDtypeStruct((taps, width), jnp.bfloat16),
+        in_specs=[pl.BlockSpec(memory_space=pltpu.VMEM)],
+        out_specs=pl.BlockSpec(memory_space=pltpu.VMEM),
+        scratch_shapes=[
+            pltpu.VMEM((n, taps, width), jnp.float32),
+            pltpu.SemaphoreType.DMA((n,)),
+            pltpu.SemaphoreType.DMA((n,)),
+        ],
+        compiler_params=pltpu.CompilerParams(collective_id=0, has_side_effects=True),
+    )(parts)
 
 
 def passed_along(value, axis, steps):
@@ -141,8 +209,10 @@
     grad_act = depthwise(jnp.concatenate([grad_b, later], 0), filter_taps)
     input_grad = (grad_u + grad_act * gate_pre).astype(jnp.bfloat16)[None]
     tap_part = depthwise(extended, grad_b)[::-1]
-    own_taps = lax.psum_scatter(tap_part, "ctx", scatter_dimension=1, tiled=True)
-    mid_grad = (own_taps * scale).astype(jnp.bfloat16)[None]
+    devices = lax.axis_size("ctx")
+    columns = tap_part.shape[1] // devices
+    parts = tap_part.reshape(tap_part.shape[0], devices, columns).transpose(1, 0, 2)
+    mid_grad = tap_exchange(parts, scale)[None]
     return (input_grad, long_grad, mid_grad)
 
 

time: 424 us -> 427 us (level)
  the two profiles are of different devices: /device:TPU:8 before, /device:TPU:95 now
where the time goes in v2:
time: 427 us; the launch traced here: 420 us
  matrix products  117 us (27%)
  Pallas kernels  116 us (27%)
  waiting for transfers between devices  75.1 us (18%)
  starting transfers between devices  42 us (10%)
  local copies, waits for them, and re-layouts  36.8 us (9%)
  other arithmetic  31 us (7%)
    pallas_call x1, Pallas kernels, tap_exchange(): pl.pallas_call(functools.partial(tap_exchange_kernel, n, scale), out_shap...  116 us
    conv_general_dilated x3, matrix products, depthwise(): lax.conv_general_dilated(extended[None], kernel[:, None, :], (1,), 'VALID...  86.3 us
    dot_general x6, matrix products, contract(): jnp.einsum(form, left, right, precision=lax.Precision.HIGH, preferred_ele...  31 us
    ppermute x1, waiting for transfers between devices, passed_along(): return lax.ppermute(value, axis, pairs)  25.3 us
    all_to_all x1, waiting for transfers between devices, per_device(): lax.all_to_all(input_part.astype(jnp.bfloat16), 'ctx', split_axis=1, conc...  24.4 us
    rev x2, local copies, waits for them, and re-layouts, per_device(): tap_part = depthwise(extended, grad_b)[::-1]  18.5 us
    all_to_all x1, waiting for transfers between devices, per_device(): lax.all_to_all(grad_z.T, 'ctx', split_axis=0, concat_axis=1, tiled=True)  14.5 us
    all_to_all x1, starting transfers between devices, per_device(): lax.all_to_all(long_in.T, 'ctx', split_axis=0, concat_axis=1, tiled=True)  12.6 us
  transfers between devices with their start and end apart: 6, of which 4 were waited for; matrix products, arithmetic and copies ran while one was open for 17% of the time, Pallas kernels for 28%

profile of v2, /device:TPU:95, one launch (start us, length us, event | category | flops | bytes accessed | tf_op | source)
XLA Modules:
  0.0 419.7 jit_solution(14151186357124783857)
XLA Ops:
  3.8 4.0 collective-permute-start.1
  9.0 10.8 %collective-permute-done.1 = bf16[127,4096]{1,0:T(8,128)(2,1)} collective-permute-done((bf16[127,4096]{1,0:T(8,128)(2,1)}, bf16[127,4096]{1,0:T(8,128)(2,1)}, u32[]{:S(2)}, u32[]{:S(2)}) %collective-permute-start.1) | collective-permute-done | bytes 1040416 | tf_op jit(solution)/shard_map/ppermute | solution.py:86
  21.4 27.4 %convolution_multiply_fusion = f32[1,128,4096]{2,0,1:T(1,128)S(1)} fusion(bf16[1,255,4096]{2,1,0:T(8,128)(2,1)S(1)} %maximum_bitcast_fusion.13, bf16[128,1,4096]{2,0,1:T(8,128)(2,1)S(1)} %bitcast.191), kind=kOutput, calls=%fused_computation.15 | convolution fusion | flops 134742016 | bytes 5234688 | tf_op jit(solution)/shard_map/conv_general_dilated | solution.py:150
  52.3 12.6 %all-to-all-start.1 = ((bf16[64,64,128]{2,1,0:T(8,128)(2,1)}), bf16[64,64,128]{2,1,0:T(8,128)(2,1)S(1)}, u32[]{:S(2)}, u32[]{:S(2)}) async-start(bf16[64,64,128]{2,1,0:T(8,128)(2,1)} %bitcast.35), calls=%async_computation.1 | async-start | bytes 2097152 | tf_op jit(solution)/shard_map/all_to_all | solution.py:187
  65.5 25.3 %collective-permute-done = bf16[128,4096]{1,0:T(8,128)(2,1)S(1)} collective-permute-done((bf16[128,4096]{1,0:T(8,128)(2,1)}, bf16[128,4096]{1,0:T(8,128)(2,1)S(1)}, u32[]{:S(2)}, u32[]{:S(2)}) %collective-permute-start) | collective-permute-done | bytes 1048608 | tf_op jit(solution)/shard_map/ppermute | solution.py:80
  94.0 12.0 %all-to-all-start = ((bf16[64,64,128]{2,1,0:T(8,128)(2,1)}), bf16[64,64,128]{2,1,0:T(8,128)(2,1)}, u32[]{:S(2)}, u32[]{:S(2)}) async-start(bf16[64,64,128]{2,1,0:T(8,128)(2,1)} %bitcast.186), calls=%async_computation | async-start | bytes 2097152 | tf_op jit(solution)/shard_map/all_to_all | solution.py:186
  111.2 5.7 %convolution_bitcast_fusion.1 = f32[64,2,128,128]{2,3,1,0:T(8,128)} fusion(bf16[64,1,64,128]{3,2,1,0:T(8,128)(2,1)S(1)} %bitcast.187, bf16[64,1,64,128]{3,2,1,0:T(8,128)(2,1)S(1)} %bitcast.188, f32[1,2,128,64]{2,3,0,1:T(8,128)S(1)} %get-tuple-element.33, f32[1,2,128,64]{2,3,0,1:T(8,128)S(1)} %get-tuple-element.32), kind=kOutput, calls=%fused_computation.34 | convolution fusion | flops 1614839808 | bytes 10616832 | tf_op jit(solution)/shard_map/qrca,nrab->nqcb/dot_general | solution.py:97
  116.9 14.5 %all-to-all-done = bf16[64,64,128]{2,1,0:T(8,128)(2,1)} async-done(((bf16[64,64,128]{2,1,0:T(8,128)(2,1)}), bf16[64,64,128]{2,1,0:T(8,128)(2,1)}, u32[]{:S(2)}, u32[]{:S(2)}) %all-to-all-start) | async-done | bytes 1048608 | tf_op jit(solution)/shard_map/all_to_all | solution.py:186
  131.4 3.8 convolution_bitcast_fusion
  135.3 5.9 %multiply_subtract_fusion.3 = (f32[64,1,128,128]{2,3,1,0:T(8,128)}, f32[64,1,128,128]{2,3,1,0:T(8,128)}, f32[64,1,128,128]{2,3,1,0:T(8,128)S(1)}, f32[64,1,128,128]{2,3,1,0:T(8,128)}) fusion(f32[64,2,128,128]{2,3,1,0:T(8,128)S(1)} %convolution_bitcast_fusion, f32[128,128]{0,1:T(8,128)S(1)} %get-tuple-element.36, f32[128,128]{0,1:T(8,128)S(1)} %get-tuple-element.37, ...), kind=kLoop, calls=%fused_computation.24 | loop fusion | flops 12582912 | bytes 33685504 | tf_op jit(solution)/shard_map/sub | solution.py:119
  141.2 6.9 %fusion.20 = f32[64,2,128,128]{2,3,0,1:T(8,128)S(1)} fusion(f32[64,1,128,128]{2,3,1,0:T(8,128)} %get-tuple-element.17, f32[64,1,128,128]{2,3,1,0:T(8,128)} %get-tuple-element.16, f32[1,2,128,128]{2,3,0,1:T(8,128)S(1)} %get-tuple-element.23, f32[1,2,128,128]{2,3,0,1:T(8,128)S(1)} %get-tuple-element.28), kind=kOutput, calls=%fused_computation.33 | convolution fusion | flops 3223388160 | bytes 17039360 | tf_op jit(solution)/shard_map/nqcb,qpbd->npcd/dot_general | solution.py:97
  148.1 4.9 %fusion.19 = f32[64,2,128,128]{2,3,0,1:T(8,128)S(1)} fusion(f32[64,1,128,128]{2,3,1,0:T(8,128)S(1)} %get-tuple-element.26, f32[64,1,128,128]{2,3,1,0:T(8,128)S(1)} %copy-done.3, f32[1,2,128,128]{2,3,0,1:T(8,128)S(1)} %get-tuple-element.23, f32[1,2,128,128]{2,3,0,1:T(8,128)S(1)} %get-tuple-element.28), kind=kOutput, calls=%fused_computation.32 | convolution fusion | flops 3223388160 | bytes 17039360 | tf_op jit(solution)/shard_map/nqcb,qpbd->npcd/dot_general | solution.py:97
  154.9 5.0 %fusion.16 = f32[64,2,128,128]{2,3,1,0:T(8,128)S(1)} fusion(f32[64,1,128,128]{2,3,0,1:T(8,128)S(1)} %get-tuple-element.13, f32[64,1,128,128]{2,3,0,1:T(8,128)S(1)} %get-tuple-element.12, f32[1,2,128,128]{2,3,1,0:T(8,128)S(1)} %copy-done.20, f32[1,2,128,128]{2,3,1,0:T(8,128)S(1)} %copy-done.19), kind=kOutput, calls=%fused_computation.30 | convolution fusion | flops 3223388160 | bytes 17039360 | tf_op jit(solution)/shard_map/npcd,pqdb->nqcb/dot_general | solution.py:97
  161.9 4.6 %fusion.33 = bf16[64,2,64,128]{3,2,1,0:T(8,128)(2,1)S(1)} fusion(f32[64,1,128,128]{2,3,1,0:T(8,128)S(1)} %get-tuple-element.15, f32[64,1,128,128]{2,3,1,0:T(8,128)S(1)} %get-tuple-element.14, f32[1,2,64,128]{3,2,1,0:T(8,128)S(1)} %copy-done.18, f32[1,2,64,128]{3,2,1,0:T(8,128)S(1)} %copy-done.17), kind=kOutput, calls=%fused_computation.60 | convolution fusion | flops 1613791232 | bytes 10616832 | tf_op jit(solution)/shard_map/rqac,nqcb->nrab/dot_general | solution.py:97
  168.4 8.8 %all-to-all-start.2 = ((bf16[64,64,128]{2,0,1:T(8,128)(2,1)}), bf16[64,64,128]{2,0,1:T(8,128)(2,1)S(1)}, u32[]{:S(2)}, u32[]{:S(2)}) async-start(bf16[64,64,128]{2,0,1:T(8,128)(2,1)} %copy.67), calls=%async_computation.2 | async-start | bytes 2097152 | tf_op jit(solution)/shard_map/all_to_all | solution.py:203
  178.4 24.4 %all-to-all-done.2 = bf16[64,64,128]{2,0,1:T(8,128)(2,1)S(1)} async-done(((bf16[64,64,128]{2,0,1:T(8,128)(2,1)}), bf16[64,64,128]{2,0,1:T(8,128)(2,1)S(1)}, u32[]{:S(2)}, u32[]{:S(2)}) %all-to-all-start.2) | async-done | bytes 1048608 | tf_op jit(solution)/shard_map/all_to_all | solution.py:203
  206.4 3.9 fusion.23
  210.3 4.1 collective-permute-start.2
  214.4 28.8 %fusion.13 = f32[1,128,4096]{2,0,1:T(1,128)S(1)} fusion(bf16[1,255,4096]{2,1,0:T(8,128)(2,1)S(1)} %copy-done.12, bf16[128,1,4096]{2,0,1:T(8,128)(2,1)} %bitcast.72), kind=kOutput, calls=%fused_computation.27 | convolution fusion | flops 134217728 | bytes 5234688 | tf_op jit(solution)/shard_map/conv_general_dilated | solution.py:150
  243.2 3.0 copy.135
  246.2 16.6 %rev.7 = f32[128,4096]{1,0:T(8,128)} reverse(f32[128,4096]{1,0:T(8,128)} %bitcast.185), dimensions={0} | reverse | bytes 4194304 | tf_op jit(solution)/shard_map/rev | solution.py:211
  267.4 116.1 %shard_map.103 = bf16[128,64]{1,0:T(8,128)(2,1)} custom-call(f32[64,128,64]{2,1,0:T(8,128)} %bitcast.182), custom_call_target="tpu_custom_call" | custom-call | tf_op jit(solution)/shard_map/pallas_call | solution.py:63
  386.5 30.1 %fusion.11 = f32[1,128,4096]{2,0,1:T(1,128)S(1)} fusion(bf16[1,255,4096]{2,1,0:T(8,128)(2,1)S(1)} %maximum_bitcast_fusion.16, bf16[128,1,4096]{2,0,1:T(8,128)(2,1)S(1)} %bitcast.190), kind=kOutput, calls=%fused_computation.25 | convolution fusion | flops 134217728 | bytes 5234688 | tf_op jit(solution)/shard_map/conv_general_dilated | solution.py:150
  416.6 2.8 fusion.35
  (77 shorter events, 36.2 us)
Async XLA Ops:
  0.6 7.1 %copy-start.13 = (bf16[1,128,4096]{2,1,0:T(8,128)(2,1)S(1)}, bf16[1,128,4096]{2,1,0:T(8,128)(2,1)}, u32[]{:S(2)}) copy-start(bf16[1,128,4096]{2,1,0:T(8,128)(2,1)} %param.15) | copy-start | bytes 3145732
  3.8 16.1 %collective-permute-start.1 = (bf16[127,4096]{1,0:T(8,128)(2,1)}, bf16[127,4096]{1,0:T(8,128)(2,1)}, u32[]{:S(2)}, u32[]{:S(2)}) collective-permute-start(bf16[127,4096]{1,0:T(8,128)(2,1)} %slice.67), channel_id=1, source_target_pairs={{0,1},{1,2},{2,3},{3,4},{4,5},{5,6},{6,7},{7,8},{8,9},{9,10},{10,1... | collective-permute-start | bytes 3121160 | tf_op jit(solution)/shard_map/ppermute | solution.py:86
  21.4 27.5 %copy-start.11 = (bf16[1,255,4096]{2,1,0:T(8,128)(2,1)}, bf16[1,255,4096]{2,1,0:T(8,128)(2,1)S(1)}, u32[]{:S(2)}) copy-start(bf16[1,255,4096]{2,1,0:T(8,128)(2,1)S(1)} %maximum_bitcast_fusion.13) | copy-start | bytes 6266884
  21.4 27.5 %copy-start.6 = (bf16[1,128,4096]{2,1,0:T(8,128)(2,1)S(1)}, bf16[1,128,4096]{2,1,0:T(8,128)(2,1)}, u32[]{:S(2)}) copy-start(bf16[1,128,4096]{2,1,0:T(8,128)(2,1)} %param.12) | copy-start | bytes 3145732
  21.4 27.5 %copy-start.8 = (bf16[1,128,4096]{2,1,0:T(8,128)(2,1)S(1)}, bf16[1,128,4096]{2,1,0:T(8,128)(2,1)}, u32[]{:S(2)}) copy-start(bf16[1,128,4096]{2,1,0:T(8,128)(2,1)} %param.9) | copy-start | bytes 3145732
  21.4 27.5 %copy-start.9 = (bf16[1,128,4096]{2,1,0:T(8,128)(2,1)S(1)}, bf16[1,128,4096]{2,1,0:T(8,128)(2,1)}, u32[]{:S(2)}) copy-start(bf16[1,128,4096]{2,1,0:T(8,128)(2,1)} %param.11) | copy-start | bytes 3145732
  52.3 41.7 %all-to-all-start.1 = ((bf16[64,64,128]{2,1,0:T(8,128)(2,1)}), bf16[64,64,128]{2,1,0:T(8,128)(2,1)S(1)}, u32[]{:S(2)}, u32[]{:S(2)}) async-start(bf16[64,64,128]{2,1,0:T(8,128)(2,1)} %bitcast.35), calls=%async_computation.1 | async-start | bytes 2097152 | tf_op jit(solution)/shard_map/all_to_all | solution.py:187
  64.9 25.9 %collective-permute-start = (bf16[128,4096]{1,0:T(8,128)(2,1)}, bf16[128,4096]{1,0:T(8,128)(2,1)S(1)}, u32[]{:S(2)}, u32[]{:S(2)}) collective-permute-start(bf16[128,4096]{1,0:T(8,128)(2,1)} %bitcast.193), channel_id=1, source_target_pairs={{0,192},{64,0},{128,64},{192,128},{1,193},{65,1},{129,65},{193,129... | collective-permute-start | bytes 3145736 | tf_op jit(solution)/shard_map/ppermute | solution.py:80
  90.8 115.5 %copy-start.4 = (bf16[128,4096]{1,0:T(8,128)(2,1)}, bf16[128,4096]{1,0:T(8,128)(2,1)S(1)}, u32[]{:S(2)}) copy-start(bf16[128,4096]{1,0:T(8,128)(2,1)S(1)} %collective-permute-done) | copy-start | bytes 3145732
  94.0 37.4 %all-to-all-start = ((bf16[64,64,128]{2,1,0:T(8,128)(2,1)}), bf16[64,64,128]{2,1,0:T(8,128)(2,1)}, u32[]{:S(2)}, u32[]{:S(2)}) async-start(bf16[64,64,128]{2,1,0:T(8,128)(2,1)} %bitcast.186), calls=%async_computation | async-start | bytes 2097152 | tf_op jit(solution)/shard_map/all_to_all | solution.py:186
  109.1 2.1 copy-start.15
  109.1 2.1 copy-start.16
  131.4 3.8 copy-start
  141.2 7.0 %copy-start.3 = (f32[64,1,128,128]{2,3,1,0:T(8,128)S(1)}, f32[64,1,128,128]{2,3,1,0:T(8,128)}, u32[]{:S(2)}) copy-start(f32[64,1,128,128]{2,3,1,0:T(8,128)} %get-tuple-element.27) | copy-start | bytes 12582916
  159.9 1.9 copy-start.17
  168.4 34.5 %all-to-all-start.2 = ((bf16[64,64,128]{2,0,1:T(8,128)(2,1)}), bf16[64,64,128]{2,0,1:T(8,128)(2,1)S(1)}, u32[]{:S(2)}, u32[]{:S(2)}) async-start(bf16[64,64,128]{2,0,1:T(8,128)(2,1)} %copy.67), calls=%async_computation.2 | async-start | bytes 2097152 | tf_op jit(solution)/shard_map/all_to_all | solution.py:203
  206.4 36.8 %copy-start.1 = (f32[4096,128]{0,1:T(8,128)}, f32[4096,128]{0,1:T(8,128)S(1)}, u32[]{:S(2)}) copy-start(f32[4096,128]{0,1:T(8,128)S(1)} %copy.68) | copy-start | bytes 6291460
  206.4 8.0 %copy-start.12 = (bf16[1,255,4096]{2,1,0:T(8,128)(2,1)S(1)}, bf16[1,255,4096]{2,1,0:T(8,128)(2,1)}, u32[]{:S(2)}) copy-start(bf16[1,255,4096]{2,1,0:T(8,128)(2,1)} %copy-done.11) | copy-start | bytes 6266884
  210.3 174.7 %collective-permute-start.2 = (bf16[127,4096]{1,0:T(8,128)(2,1)}, bf16[127,4096]{1,0:T(8,128)(2,1)S(1)}, u32[]{:S(2)}, u32[]{:S(2)}) collective-permute-start(bf16[127,4096]{1,0:T(8,128)(2,1)} %bitcast.181), channel_id=1, source_target_pairs={{1,0},{2,1},{3,2},{4,3},{5,4},{6,5},{7,6},{8,7},{9,8},{10,9},{11,1... | collective-permute-start | bytes 3121160 | tf_op jit(solution)/shard_map/ppermute | solution.py:86
  267.4 119.0 %copy-start.14 = (bf16[1,128,4096]{2,1,0:T(8,128)(2,1)S(1)}, bf16[1,128,4096]{2,1,0:T(8,128)(2,1)}, u32[]{:S(2)}) copy-start(bf16[1,128,4096]{2,1,0:T(8,128)(2,1)} %param.15) | copy-start | bytes 3145732
  386.4 30.2 %copy-start.2 = (f32[4096,128]{0,1:T(8,128)S(1)}, f32[4096,128]{0,1:T(8,128)}, u32[]{:S(2)}) copy-start(f32[4096,128]{0,1:T(8,128)} %copy-done.1) | copy-start | bytes 6291460
  386.4 30.2 %copy-start.5 = (bf16[128,4096]{1,0:T(8,128)(2,1)S(1)}, bf16[128,4096]{1,0:T(8,128)(2,1)}, u32[]{:S(2)}) copy-start(bf16[128,4096]{1,0:T(8,128)(2,1)} %copy-done.4) | copy-start | bytes 3145732
  386.4 30.2 %copy-start.7 = (bf16[1,128,4096]{2,1,0:T(8,128)(2,1)S(1)}, bf16[1,128,4096]{2,1,0:T(8,128)(2,1)}, u32[]{:S(2)}) copy-start(bf16[1,128,4096]{2,1,0:T(8,128)(2,1)} %param.12) | copy-start | bytes 3145732
  386.5 30.2 %copy-start.10 = (bf16[1,128,4096]{2,1,0:T(8,128)(2,1)S(1)}, bf16[1,128,4096]{2,1,0:T(8,128)(2,1)}, u32[]{:S(2)}) copy-start(bf16[1,128,4096]{2,1,0:T(8,128)(2,1)} %param.10) | copy-start | bytes 3145732
  (3 other events, 5.6 us)
